TPU v7x, 32 devices: a whole 2x2x4 slice. The times are simulated.
32 devices in a mesh: seq: 4 (over y, x), ctx: 8 (over z, core).
Axes of the slice: x: 2, y: 2, z: 4, core: 2. Of those that a mesh axis runs over, the one named last changes fastest.
Arguments:
- hidden_in: bfloat16 [16, 1024, 768], P('seq', 'ctx'), may hold values from -6 to 6
- cotangent: bfloat16 [16, 1024, 768], P('seq', 'ctx'), may hold values from -6 to 6
- segments: int32 [16, 1024], P('seq', 'ctx'), may hold values from 0 to 3, never falling along the last dimension, each value on 1 to 512 neighbouring positions
- qkv_weight: bfloat16 [768, 2304], P('seq'), may hold values from -0.21875 to 0.21875
- query_bias: bfloat16 [768], P('seq'), may hold values from -3 to 3
- value_bias: bfloat16 [768], P('seq'), may hold values from -0.29882812 to 0.29882812
- out_weight: bfloat16 [768, 768], P('seq'), may hold values from -1.75 to 1.75
- out_bias: bfloat16 [768], P('seq'), may hold values from -2 to 2
- first_gain: bfloat16 [768], P('seq'), may hold values from 0.5 to 1.5
- first_shift: bfloat16 [768], P('seq'), may hold values from -2 to 2
- inner_weight: bfloat16 [768, 3072], P('seq'), may hold values from -0.21875 to 0.21875
- inner_bias: bfloat16 [3072], P('seq'), may hold values from -3 to 3
- outer_weight: bfloat16 [3072, 768], P('seq'), may hold values from -0.21875 to 0.21875
- outer_bias: bfloat16 [768], P('seq'), may hold values from -2 to 2
- second_gain: bfloat16 [768], P('seq'), may hold values from 0.5 to 1.5
- second_shift: bfloat16 [768], P('seq'), may hold values from -2 to 2
Outputs:
- output: bfloat16 [16, 1024, 768], P('seq', 'ctx')
- grad_input: float32 [16, 1024, 768], P('seq', 'ctx')
- grad_qkv_weight: float32 [768, 2304], P('seq')
- grad_query_bias: float32 [768], P('seq')
- grad_value_bias: float32 [768], P('seq')
- grad_out_weight: float32 [768, 768], P('seq')
- grad_out_bias: float32 [768], P('seq')
- grad_first_gain: float32 [768], P('seq')
- grad_first_shift: float32 [768], P('seq')
- grad_inner_weight: float32 [768, 3072], P('seq')
- grad_inner_bias: float32 [3072], P('seq')
- grad_outer_weight: float32 [3072, 768], P('seq')
- grad_outer_bias: float32 [768], P('seq')
- grad_second_gain: float32 [768], P('seq')
- grad_second_shift: float32 [768], P('seq')
Inputs may be any that keep to these rules, and one draw needn't show every extreme that they name: `segments`: in each sequence the document numbers never fall along the positions; a document holds 1 to 512 positions, and some document holds exactly 512; attention joins only positions of one document of one sequence.
All inputs are finite; a program needn't handle non-finite values.
Results may differ from a plain program's by a relative error of at most 0.035.
Values may be sent and summed in bfloat16 or wider, within the bound.
A program may use at most 320 MiB of HBM per device.

v0:
```python
from functools import partial
import jax
import jax.numpy as jnp
from jax import lax
from jax.sharding import PartitionSpec as P

HEADS = 12
HEAD_DIM = 64
norm_epsilon = 1e-12


def norm_forward(matrix, gain, shift):
    average = jnp.mean(matrix, axis=-1, keepdims=True)
    centred = matrix - average
    factor = lax.rsqrt(jnp.mean(centred * centred, axis=-1, keepdims=True) + norm_epsilon)
    normed = centred * factor
    return (normed * gain + shift, normed, factor)


def norm_backward(upstream, normed, factor, gain):
    scaled = upstream * gain
    return factor * (
        scaled
        - jnp.mean(scaled, axis=-1, keepdims=True)
        - normed * jnp.mean(scaled * normed, axis=-1, keepdims=True)
    )


def split_heads(matrix):
    groups, positions, widths = matrix.shape
    return jnp.moveaxis(matrix.reshape(groups, positions, HEADS, widths // HEADS), 2, 0)


def join_heads(matrix):
    return jnp.moveaxis(matrix, 0, 2).reshape(
        matrix.shape[1], matrix.shape[2], matrix.shape[0] * matrix.shape[3]
    )


def grads_block(query_one, upstream_one, lse_one, delta_one, key_one, value_one, allowed, scaling):
    scores = (
        jnp.einsum("sqd,skd->sqk", query_one, key_one, preferred_element_type=jnp.float32) * scaling
    )
    probability = jnp.exp(jnp.where(allowed, scores - lse_one[..., None], -1e30))
    grad_probs = jnp.einsum(
        "sqd,skd->sqk", upstream_one, value_one, preferred_element_type=jnp.float32
    )
    grad_scores = (probability * (grad_probs - delta_one[..., None])).astype(jnp.bfloat16)
    grad_query = (
        jnp.einsum("sqk,skd->sqd", grad_scores, key_one, preferred_element_type=jnp.float32)
        * scaling
    )
    grad_key = (
        jnp.einsum("sqk,sqd->skd", grad_scores, query_one, preferred_element_type=jnp.float32)
        * scaling
    )
    grad_value = jnp.einsum(
        "sqk,sqd->skd",
        probability.astype(jnp.bfloat16),
        upstream_one,
        preferred_element_type=jnp.float32,
    )
    return (grad_query, grad_key, grad_value)


def on_device(
    hidden_in,
    cotangent,
    segments,
    qkv_weight,
    query_bias,
    value_bias,
    out_weight,
    out_bias,
    first_gain,
    first_shift,
    inner_weight,
    inner_bias,
    outer_weight,
    outer_bias,
    second_gain,
    second_shift,
):
    groups, positions, model_width = hidden_in.shape
    row_count = groups * positions
    scaling = HEAD_DIM ** (-0.5)
    gathered = (
        lax.all_gather(qkv_weight, "seq", axis=0, tiled=True),
        lax.all_gather(query_bias, "seq", axis=0, tiled=True),
        lax.all_gather(value_bias, "seq", axis=0, tiled=True),
        lax.all_gather(out_weight, "seq", axis=0, tiled=True),
        lax.all_gather(out_bias, "seq", axis=0, tiled=True),
        lax.all_gather(first_gain, "seq", axis=0, tiled=True),
        lax.all_gather(first_shift, "seq", axis=0, tiled=True),
        lax.all_gather(inner_weight, "seq", axis=0, tiled=True),
        lax.all_gather(inner_bias, "seq", axis=0, tiled=True),
        lax.all_gather(outer_weight, "seq", axis=0, tiled=True),
        lax.all_gather(outer_bias, "seq", axis=0, tiled=True),
        lax.all_gather(second_gain, "seq", axis=0, tiled=True),
        lax.all_gather(second_shift, "seq", axis=0, tiled=True),
    )
    (
        qkv_full,
        qbias_full,
        vbias_full,
        out_full,
        obias_full,
        fgain_full,
        fshift_full,
        inner_full,
        ibias_full,
        outer_full,
        ubias_full,
        sgain_full,
        sshift_full,
    ) = gathered
    token_rows = hidden_in.reshape(row_count, model_width)
    projected = jnp.dot(token_rows, qkv_full, preferred_element_type=jnp.float32)
    queries_low = (
        (projected[:, :model_width] + qbias_full)
        .astype(jnp.bfloat16)
        .reshape(groups, positions, model_width)
    )
    keys_low = (
        projected[:, model_width : 2 * model_width]
        .astype(jnp.bfloat16)
        .reshape(groups, positions, model_width)
    )
    values_low = (
        (projected[:, 2 * model_width :] + vbias_full)
        .astype(jnp.bfloat16)
        .reshape(groups, positions, model_width)
    )
    seg_low = segments.astype(jnp.bfloat16)
    query_heads = split_heads(queries_low)
    start_state = (
        jnp.full((HEADS, groups, positions), -1e30, jnp.float32),
        jnp.zeros((HEADS, groups, positions), jnp.float32),
        jnp.zeros((HEADS, groups, positions, HEAD_DIM), jnp.float32),
    )
    key_part = lax.all_gather(keys_low, "ctx", axis=1, tiled=True)
    value_part = lax.all_gather(values_low, "ctx", axis=1, tiled=True)
    seg_part = lax.all_gather(seg_low, "ctx", axis=1, tiled=True)
    fold_allowed = seg_low[:, :, None] == seg_part[:, None, :]

    def per_head(head_item):
        query_one, key_one, value_one, old_max, old_total, old_acc = head_item
        scores = (
            jnp.einsum("sqd,skd->sqk", query_one, key_one, preferred_element_type=jnp.float32)
            * scaling
        )
        scores = jnp.where(fold_allowed, scores, -1e30)
        new_max = jnp.maximum(old_max, jnp.max(scores, axis=-1))
        retain = jnp.exp(old_max - new_max)
        weights = jnp.where(fold_allowed, jnp.exp(scores - new_max[..., None]), 0.0)
        run_total = old_total * retain + jnp.sum(weights, axis=-1)
        run_acc = old_acc * retain[..., None] + jnp.einsum(
            "sqk,skd->sqd",
            weights.astype(jnp.bfloat16),
            value_one,
            preferred_element_type=jnp.float32,
        )
        return (new_max, run_total, run_acc)

    run_max, run_total, run_acc = lax.map(
        per_head,
        (
            query_heads,
            split_heads(key_part),
            split_heads(value_part),
            start_state[0],
            start_state[1],
            start_state[2],
        ),
    )
    out_heads = run_acc / run_total[..., None]
    row_lse = run_max + jnp.log(run_total)
    context_low = join_heads(out_heads).reshape(row_count, model_width).astype(jnp.bfloat16)
    attended = jnp.dot(context_low, out_full, preferred_element_type=jnp.float32) + obias_full
    residual = token_rows.astype(jnp.float32) + attended
    first, first_normed, first_factor = norm_forward(residual, fgain_full, fshift_full)
    first_low = first.astype(jnp.bfloat16)
    inner = jnp.dot(first_low, inner_full, preferred_element_type=jnp.float32) + ibias_full
    active = jax.nn.gelu(inner, approximate=False).astype(jnp.bfloat16)
    branch = jnp.dot(active, outer_full, preferred_element_type=jnp.float32) + ubias_full
    result, second_normed, second_factor = norm_forward(first + branch, sgain_full, sshift_full)
    output = result.astype(jnp.bfloat16).reshape(groups, positions, model_width)
    qkv_back, out_back, inner_back, outer_back, fgain_back, sgain_back = (
        lax.all_gather(qkv_weight, "seq", axis=0, tiled=True),
        lax.all_gather(out_weight, "seq", axis=0, tiled=True),
        lax.all_gather(inner_weight, "seq", axis=0, tiled=True),
        lax.all_gather(outer_weight, "seq", axis=0, tiled=True),
        lax.all_gather(first_gain, "seq", axis=0, tiled=True),
        lax.all_gather(second_gain, "seq", axis=0, tiled=True),
    )
    grad_out = cotangent.reshape(row_count, model_width).astype(jnp.float32)
    grad_second_gain = jnp.sum(grad_out * second_normed, axis=0)
    grad_second_shift = jnp.sum(grad_out, axis=0)
    grad_second = norm_backward(grad_out, second_normed, second_factor, sgain_back)
    grad_branch = grad_second.astype(jnp.bfloat16)
    grad_outer_weight = jnp.einsum(
        "rf,rd->fd", active, grad_branch, preferred_element_type=jnp.float32
    )
    grad_outer_bias = jnp.sum(grad_branch.astype(jnp.float32), axis=0)
    grad_active = jnp.einsum(
        "rd,fd->rf", grad_branch, outer_back, preferred_element_type=jnp.float32
    )
    _, gelu_pull = jax.vjp(partial(jax.nn.gelu, approximate=False), inner)
    grad_inner = gelu_pull(grad_active)[0].astype(jnp.bfloat16)
    grad_inner_weight = jnp.einsum(
        "rd,rf->df", first_low, grad_inner, preferred_element_type=jnp.float32
    )
    grad_inner_bias = jnp.sum(grad_inner.astype(jnp.float32), axis=0)
    grad_first = grad_second + jnp.einsum(
        "rf,df->rd", grad_inner, inner_back, preferred_element_type=jnp.float32
    )
    grad_first_gain = jnp.sum(grad_first * first_normed, axis=0)
    grad_first_shift = jnp.sum(grad_first, axis=0)
    grad_residual = norm_backward(grad_first, first_normed, first_factor, fgain_back)
    grad_attended = grad_residual.astype(jnp.bfloat16)
    grad_out_weight = jnp.einsum(
        "rd,re->de", context_low, grad_attended, preferred_element_type=jnp.float32
    )
    grad_out_bias = jnp.sum(grad_attended.astype(jnp.float32), axis=0)
    grad_context = jnp.einsum(
        "re,de->rd", grad_attended, out_back, preferred_element_type=jnp.float32
    )
    grad_context = grad_context.astype(jnp.bfloat16).reshape(groups, positions, model_width)
    grad_heads = split_heads(grad_context)
    row_delta = jnp.sum(grad_heads.astype(jnp.float32) * out_heads, axis=-1)
    far_keys, far_values, far_segs = (
        lax.all_gather(keys_low, "ctx", axis=1, tiled=True),
        lax.all_gather(values_low, "ctx", axis=1, tiled=True),
        lax.all_gather(seg_low, "ctx", axis=1, tiled=True),
    )
    allowed = seg_low[:, :, None] == far_segs[:, None, :]

    def head_keys(head_item):
        query_one, upstream_one, lse_one, delta_one, key_one, value_one = head_item
        return grads_block(
            query_one, upstream_one, lse_one, delta_one, key_one, value_one, allowed, scaling
        )

    dq_heads, dk_heads, dv_heads = lax.map(
        head_keys,
        (
            query_heads,
            grad_heads,
            row_lse,
            row_delta,
            split_heads(far_keys),
            split_heads(far_values),
        ),
    )
    key_grad, value_grad = (
        lax.psum_scatter(
            join_heads(dk_heads).astype(jnp.bfloat16), "ctx", scatter_dimension=1, tiled=True
        ).astype(jnp.float32),
        lax.psum_scatter(
            join_heads(dv_heads).astype(jnp.bfloat16), "ctx", scatter_dimension=1, tiled=True
        ).astype(jnp.float32),
    )
    query_grad = join_heads(dq_heads)
    query_low_grad = query_grad.reshape(row_count, model_width).astype(jnp.bfloat16)
    key_low_grad = key_grad.reshape(row_count, model_width).astype(jnp.bfloat16)
    value_low_grad = value_grad.reshape(row_count, model_width).astype(jnp.bfloat16)
    grad_projected = jnp.concatenate([query_low_grad, key_low_grad, value_low_grad], axis=1)
    grad_qkv_weight = jnp.einsum(
        "rd,rf->df", token_rows, grad_projected, preferred_element_type=jnp.float32
    )
    grad_query_bias = jnp.sum(query_low_grad.astype(jnp.float32), axis=0)
    grad_value_bias = jnp.sum(value_low_grad.astype(jnp.float32), axis=0)
    grad_input = grad_residual + jnp.einsum(
        "rf,df->rd", grad_projected, qkv_back, preferred_element_type=jnp.float32
    )
    owned = (
        lax.psum_scatter(
            grad_qkv_weight.astype(jnp.bfloat16), "seq", scatter_dimension=0, tiled=True
        ).astype(jnp.float32),
        lax.psum_scatter(
            grad_query_bias.astype(jnp.bfloat16), "seq", scatter_dimension=0, tiled=True
        ).astype(jnp.float32),
        lax.psum_scatter(
            grad_value_bias.astype(jnp.bfloat16), "seq", scatter_dimension=0, tiled=True
        ).astype(jnp.float32),
        lax.psum_scatter(
            grad_out_weight.astype(jnp.bfloat16), "seq", scatter_dimension=0, tiled=True
        ).astype(jnp.float32),
        lax.psum_scatter(
            grad_out_bias.astype(jnp.bfloat16), "seq", scatter_dimension=0, tiled=True
        ).astype(jnp.float32),
        lax.psum_scatter(
            grad_first_gain.astype(jnp.bfloat16), "seq", scatter_dimension=0, tiled=True
        ).astype(jnp.float32),
        lax.psum_scatter(
            grad_first_shift.astype(jnp.bfloat16), "seq", scatter_dimension=0, tiled=True
        ).astype(jnp.float32),
        lax.psum_scatter(
            grad_inner_weight.astype(jnp.bfloat16), "seq", scatter_dimension=0, tiled=True
        ).astype(jnp.float32),
        lax.psum_scatter(
            grad_inner_bias.astype(jnp.bfloat16), "seq", scatter_dimension=0, tiled=True
        ).astype(jnp.float32),
        lax.psum_scatter(
            grad_outer_weight.astype(jnp.bfloat16), "seq", scatter_dimension=0, tiled=True
        ).astype(jnp.float32),
        lax.psum_scatter(
            grad_outer_bias.astype(jnp.bfloat16), "seq", scatter_dimension=0, tiled=True
        ).astype(jnp.float32),
        lax.psum_scatter(
            grad_second_gain.astype(jnp.bfloat16), "seq", scatter_dimension=0, tiled=True
        ).astype(jnp.float32),
        lax.psum_scatter(
            grad_second_shift.astype(jnp.bfloat16), "seq", scatter_dimension=0, tiled=True
        ).astype(jnp.float32),
    )
    summed = (
        lax.psum(owned[0].astype(jnp.bfloat16), "ctx").astype(jnp.float32),
        lax.psum(owned[1].astype(jnp.bfloat16), "ctx").astype(jnp.float32),
        lax.psum(owned[2].astype(jnp.bfloat16), "ctx").astype(jnp.float32),
        lax.psum(owned[3].astype(jnp.bfloat16), "ctx").astype(jnp.float32),
        lax.psum(owned[4].astype(jnp.bfloat16), "ctx").astype(jnp.float32),
        lax.psum(owned[5].astype(jnp.bfloat16), "ctx").astype(jnp.float32),
        lax.psum(owned[6].astype(jnp.bfloat16), "ctx").astype(jnp.float32),
        lax.psum(owned[7].astype(jnp.bfloat16), "ctx").astype(jnp.float32),
        lax.psum(owned[8].astype(jnp.bfloat16), "ctx").astype(jnp.float32),
        lax.psum(owned[9].astype(jnp.bfloat16), "ctx").astype(jnp.float32),
        lax.psum(owned[10].astype(jnp.bfloat16), "ctx").astype(jnp.float32),
        lax.psum(owned[11].astype(jnp.bfloat16), "ctx").astype(jnp.float32),
        lax.psum(owned[12].astype(jnp.bfloat16), "ctx").astype(jnp.float32),
    )
    return (
        output,
        grad_input.reshape(groups, positions, model_width),
        summed[0],
        summed[1],
        summed[2],
        summed[3],
        summed[4],
        summed[5],
        summed[6],
        summed[7],
        summed[8],
        summed[9],
        summed[10],
        summed[11],
        summed[12],
    )


def solution(mesh):
    placed = (
        P("seq", "ctx", None),
        P("seq", "ctx", None),
        P("seq", "ctx"),
        P("seq", None),
        P("seq"),
        P("seq"),
        P("seq", None),
        P("seq"),
        P("seq"),
        P("seq"),
        P("seq", None),
        P("seq"),
        P("seq", None),
        P("seq"),
        P("seq"),
        P("seq"),
    )
    return jax.shard_map(
        on_device,
        mesh=mesh,
        in_specs=placed,
        out_specs=(
            P("seq", "ctx", None),
            P("seq", "ctx", None),
            P("seq", None),
            P("seq"),
            P("seq"),
            P("seq", None),
            P("seq"),
            P("seq"),
            P("seq"),
            P("seq", None),
            P("seq"),
            P("seq", None),
            P("seq"),
            P("seq"),
            P("seq"),
        ),
        check_vma=False,
    )
```

profile of v0, /device:TPU:0, one launch (start us, length us, event | category | flops | bytes accessed | tf_op | source)
XLA Modules:
  0.0 961.4 jit_solution(5188691105644556815)
XLA Ops:
  15.8 17.8 %all-reduce.20 = (bf16[768]{0:T(1024)(128)(2,1)S(1)}, bf16[768]{0:T(1024)(128)(2,1)S(1)}, bf16[768]{0:T(1024)(128)(2,1)S(1)}, bf16[768]{0:T(1024)(128)(2,1)S(1)}...) all-reduce(bf16[768]{0:T(1024)(128)(2,1)S(1)} %dynamic-update-slice, ...), channel_id=1, replica_groups=mesh['seq'=4,'ctx'=8] {'seq'}, use_global_device_ids=true, to_apply=%add | all-reduce | flops 5376 | bytes 21504
  33.7 26.3 %all-gather.8.cloned.1.call-done = bf16[768,2304]{1,0:T(8,128)(2,1)} async-done(((bf16[192,2304]{1,0:T(8,128)(2,1)}), bf16[768,2304]{1,0:T(8,128)(2,1)}) %all-gather.8.cloned.1.call-update) | async-done | bytes 3538960 | tf_op jit(solution)/shard_map/all_gather | solution.py:88
  60.0 4.3 fusion.86
  72.2 11.9 %all_gather.60 = bf16[4,1024]{1,0:T(4,128)(2,1)S(1)} all-gather(bf16[4,128]{1,0:T(4,128)(2,1)S(1)} %convert_element_type.236), channel_id=1, replica_groups=mesh['seq'=4,'ctx'=8] {'ctx'}, dimensions={1}, use_global_device_ids=true | all-gather | bytes 9216 | tf_op jit(solution)/shard_map/all_gather | solution.py:143
  84.1 8.2 all-gather
  96.5 36.3 %all-gather.12.cloned.1.call-done = bf16[4,1024,768]{1,2,0:T(8,128)(2,1)} async-done(((bf16[4,128,768]{1,2,0:T(8,128)(2,1)}), bf16[4,1024,768]{1,2,0:T(8,128)(2,1)}) %all-gather.12.cloned.1.call-update) | async-done | bytes 6291472 | tf_op jit(solution)/shard_map/all_gather | solution.py:142
  132.9 6.7 copy.57
  139.6 58.8 %all-gather.10.cloned.1.call-done = bf16[4,1024,768]{1,2,0:T(8,128)(2,1)} async-done(((bf16[4,128,768]{1,2,0:T(8,128)(2,1)}), bf16[4,1024,768]{1,2,0:T(8,128)(2,1)}) %all-gather.10.cloned.1.call-update) | async-done | bytes 6291472 | tf_op jit(solution)/shard_map/all_gather | solution.py:141
  198.4 6.7 copy.56
  205.1 51.8 %while.30 = (s32[]{:T(128)}, f32[12,4,128]{2,1,0:T(4,128)S(1)}, f32[12,4,128]{2,1,0:T(4,128)S(1)}, f32[12,4,128,64]{2,1,3,0:T(4,128)S(1)}, bf16[12,4,128,64]{2,3...) while((s32[]{:T(128)}, f32[12,4,128]{2,1,0:T(4,128)S(1)}, ...), condition=%wide.region_3.4_spmd.clone, body=%wide.region_0.3_spmd.clone.sunk | while | flops 142641664 | bytes 7852653 | solution.py:165
  258.0 2.6 fusion.83
  261.0 23.9 %all-gather.16.cloned.1.call-done = bf16[768,3072]{1,0:T(8,128)(2,1)} async-done(((bf16[192,3072]{1,0:T(8,128)(2,1)}), bf16[768,3072]{1,0:T(8,128)(2,1)}) %all-gather.16.cloned.1.call-update) | async-done | bytes 4718608 | tf_op jit(solution)/shard_map/all_gather | solution.py:95
  284.9 19.8 %multiply_convert_fusion.1 = (bf16[512,3072]{1,0:T(8,128)(2,1)}, f32[512,3072]{1,0:T(8,128)}, f32[512,3072]{1,0:T(8,128)}) fusion(f32[3072]{0:T(1024)S(1)} %bitcast.237, bf16[768,3072]{1,0:T(8,128)(2,1)} %all-gather.16.cloned.1.call-done, f32[512,768]{1,0:T(8,128)S(1)} %get-tuple-element.358, f32[768]{0:T(1024)S(1)} %convert_element_type.244, ...), kind=kOutput, calls=%fused_computation.66 | convolution fusion | flops 2521694208 | bytes 22042624 | tf_op jit(solution)/shard_map/dot_general | solution.py:183
  304.7 39.0 %all-gather.18.cloned.1.call-done = bf16[3072,768]{1,0:T(8,128)(2,1)} async-done(((bf16[768,768]{1,0:T(8,128)(2,1)}), bf16[3072,768]{1,0:T(8,128)(2,1)}) %all-gather.18.cloned.1.call-update) | async-done | bytes 4718608 | tf_op jit(solution)/shard_map/all_gather | solution.py:97
  343.7 6.5 fusion.84
  353.2 9.2 fusion.85
  362.4 5.1 multiply_reduce_fusion
  375.0 103.3 %while.31 = (s32[]{:T(128)}, bf16[12,4,128,64]{2,3,1,0:T(8,128)(2,1)}, bf16[12,4,1024,64]{2,3,0,1:T(8,128)(2,1)}, bf16[12,4,1024,64]{2,3,0,1:T(8,128)(2,1)}, bf1...) while((s32[]{:T(128)}, ...), condition=%wide.region_14.15_spmd.clone, body=%wide.region_13.14_spmd.clone.sunk | while | flops 340033536 | bytes 13657221 | solution.py:244
  378.8 2.0 fusion.139
  381.8 2.2 fusion.138
  390.4 2.2 fusion.138
  395.9 1.9 fusion.139
  398.9 2.2 fusion.138
  404.5 1.9 fusion.139
  407.5 2.2 fusion.138
  413.1 1.9 fusion.139
  416.1 2.2 fusion.138
  421.6 2.0 fusion.139
  424.6 2.2 fusion.138
  430.2 2.0 fusion.139
  433.2 2.2 fusion.138
  438.7 2.0 fusion.139
  441.8 2.2 fusion.138
  450.4 2.2 fusion.138
  455.9 2.0 fusion.139
  458.9 2.2 fusion.138
  467.5 2.2 fusion.138
  473.0 2.0 fusion.139
  476.1 2.2 fusion.138
  478.3 10.8 %copy.70 = bf16[4,1024,768]{2,0,1:T(4,128)(2,1)} copy(bf16[4,1024,768]{1,2,0:T(8,128)(2,1)} %bitcast.219) | data formatting | bytes 12582912
  489.0 6.9 copy.100
  496.0 11.0 %copy.72 = bf16[4,1024,768]{2,0,1:T(4,128)(2,1)} copy(bf16[4,1024,768]{1,2,0:T(8,128)(2,1)} %bitcast.220) | data formatting | bytes 12582912
  507.0 7.0 copy.102
  516.8 49.2 %reduce-scatter.19.cloned.1.call-done = bf16[128,3072]{1,0:T(8,128)(2,1)} async-done(((bf16[1024,3072]{1,0:T(8,128)(2,1)}), bf16[128,3072]{1,0:T(8,128)(2,1)}) %reduce-scatter.19.cloned.1.call-update) | async-done | bytes 786448
  565.9 2.0 reshape.221
  569.3 67.2 %reduce-scatter.21.cloned.1.call-done = bf16[128,3072]{1,0:T(8,128)(2,1)} async-done(((bf16[1024,3072]{1,0:T(8,128)(2,1)}), bf16[128,3072]{1,0:T(8,128)(2,1)}) %reduce-scatter.21.cloned.1.call-update) | async-done | bytes 786448
  636.5 2.0 reshape.223
  639.8 2.2 bitcast_dynamic-update-slice_fusion.2
  642.0 2.1 bitcast_dynamic-update-slice_fusion.1
  644.1 5.4 fusion.54
  649.5 5.8 copy.74
  655.4 3.5 convolution_convert_fusion.3
  659.1 7.9 convolution_convert_fusion.1
  667.2 7.4 convolution_convert_fusion
  674.7 26.5 %reduce-scatter.23.cloned.1.call-done = bf16[192,2304]{1,0:T(8,128)(2,1)} async-done(((bf16[768,2304]{1,0:T(8,128)(2,1)}), bf16[192,2304]{1,0:T(8,128)(2,1)}) %reduce-scatter.23.cloned.1.call-update) | async-done | bytes 884752
  701.1 2.3 copy.75
  703.5 29.0 %reduce-scatter.13.cloned.1.call-done = bf16[192,768]{1,0:T(8,128)(2,1)} async-done(((bf16[768,768]{1,0:T(8,128)(2,1)}), bf16[192,768]{1,0:T(8,128)(2,1)}) %reduce-scatter.13.cloned.1.call-update) | async-done | bytes 294928 | tf_op jit(solution)/shard_map/reduce_scatter | solution.py:286
  732.5 60.1 %reduce-scatter.15.cloned.1.call-done = bf16[192,3072]{1,0:T(8,128)(2,1)} async-done(((bf16[768,3072]{1,0:T(8,128)(2,1)}), bf16[192,3072]{1,0:T(8,128)(2,1)}) %reduce-scatter.15.cloned.1.call-update) | async-done | bytes 1179664 | tf_op jit(solution)/shard_map/reduce_scatter | solution.py:298
  792.6 60.0 %reduce-scatter.17.cloned.1.call-done = bf16[768,768]{1,0:T(8,128)(2,1)} async-done(((bf16[3072,768]{1,0:T(8,128)(2,1)}), bf16[768,768]{1,0:T(8,128)(2,1)}) %reduce-scatter.17.cloned.1.call-update) | async-done | bytes 1179664 | tf_op jit(solution)/shard_map/reduce_scatter | solution.py:304
  856.1 15.5 %all-reduce.19 = (bf16[768]{0:T(1024)(128)(2,1)S(1)}, bf16[768]{0:T(1024)(128)(2,1)S(1)}, bf16[768]{0:T(1024)(128)(2,1)S(1)}, bf16[768]{0:T(1024)(128)(2,1)S(1)}...) all-reduce(bf16[768]{0:T(1024)(128)(2,1)S(1)} %dynamic-update-slice, ...), channel_id=1, replica_groups=mesh['seq'=4,'ctx'=8] {'seq'}, use_global_device_ids=true, to_apply=%add.7 | all-reduce | flops 9984 | bytes 39936
  872.3 15.2 %all-reduce.17 = (bf16[192]{0:T(256)(128)(2,1)S(1)}, bf16[192]{0:T(256)(128)(2,1)S(1)}, bf16[192]{0:T(256)(128)(2,1)S(1)}, bf16[192]{0:T(256)(128)(2,1)S(1)}, bf...) all-reduce(bf16[192]{0:T(256)(128)(2,1)S(1)} %dynamic-slice.9, ...), channel_id=1, replica_groups=mesh['seq'=4,'ctx'=8] {'ctx'}, use_global_device_ids=true, to_apply=%region_21.22 | all-reduce | flops 2304 | bytes 9216 | tf_op jit(solution)/shard_map/psum | solution.py:319
  893.8 5.9 convolution_add_fusion.1
  899.7 47.9 %all-reduce.23.cloned.1.call-done = (bf16[192,2304]{0,1:T(8,128)(2,1)}, bf16[192,768]{1,0:T(8,128)(2,1)}, bf16[192,3072]{1,0:T(8,128)(2,1)}, bf16[768,768]{1,0:T(8,128)(2,1)}) async-done(((bf16[192,2304]{0,1:T(8,128)(2,1)}, bf16[192,768]{1,0:T(8,128)(2,1)}, bf16[192,3072]{1,0:T(8,128)(2,1)}, bf16[768,768]{1,0:T(8,128)(2,1)}), (bf16[192,2304]{0,1:T(8,128)(2,1)}, bf16[192,768]{1,0:T(8,128)(2,1)}, ...) | async-done | bytes 3538960 | tf_op jit(solution)/shard_map/psum | solution.py:318
  947.6 3.0 convert_element_type.284
  (293 shorter events, 161.5 us)
Async XLA Ops:
  7.2 52.8 %all-gather.8.cloned.1.call-start = ((), (), s32[]{:S(2)}) async-start(), calls=%async_computation.6 | async-start | bytes 4423680 | tf_op jit(solution)/shard_map/all_gather | solution.py:88
  7.9 125.0 %all-gather.12.cloned.1.call-start = ((), (), s32[]{:S(2)}) async-start(), calls=%async_computation.8 | async-start | bytes 7077888 | tf_op jit(solution)/shard_map/all_gather | solution.py:142
  64.2 2.1 copy-start.6
  67.5 130.9 %all-gather.10.cloned.1.call-start = ((), (), s32[]{:S(2)}) async-start(), calls=%async_computation.7 | async-start | bytes 7077888 | tf_op jit(solution)/shard_map/all_gather | solution.py:141
  69.1 3.1 copy-start.12
  69.1 15.0 %copy-start.13 = (bf16[768]{0:T(1024)(128)(2,1)S(1)}, bf16[768]{0:T(1024)(128)(2,1)}, u32[]{:S(2)}) copy-start(bf16[768]{0:T(1024)(128)(2,1)} %param.31) | copy-start | bytes 4612
  69.1 23.2 %copy-start = (bf16[4,128,768]{2,1,0:T(8,128)(2,1)S(1)}, bf16[4,128,768]{2,1,0:T(8,128)(2,1)}, u32[]{:S(2)}) copy-start(bf16[4,128,768]{2,1,0:T(8,128)(2,1)} %param.21) | copy-start | bytes 2359300
  70.3 187.0 %all-gather.14.cloned.1.call-start = ((), (), s32[]{:S(2)}) async-start(), calls=%async_computation.9 | async-start | bytes 1474560 | tf_op jit(solution)/shard_map/all_gather | solution.py:91
  70.9 214.0 %all-gather.16.cloned.1.call-start = ((), (), s32[]{:S(2)}) async-start(), calls=%async_computation.10 | async-start | bytes 5898240 | tf_op jit(solution)/shard_map/all_gather | solution.py:95
  71.5 272.2 %all-gather.18.cloned.1.call-start = ((), (), s32[]{:S(2)}) async-start(), calls=%async_computation.11 | async-start | bytes 5898240 | tf_op jit(solution)/shard_map/all_gather | solution.py:97
  72.0 493.9 %reduce-scatter.19.cloned.1.call-start = ((), (), s32[]{:S(2)}) async-start(), calls=%async_computation.15 | async-start | bytes 7077888
  256.9 1.1 copy-start.5
  257.2 3.4 copy-start.7
  260.7 44.0 %copy-start.3 = (f32[512,768]{1,0:T(8,128)}, f32[512,768]{1,0:T(8,128)S(1)}, u32[]{:S(2)}) copy-start(f32[512,768]{1,0:T(8,128)S(1)} %get-tuple-element.358) | copy-start | bytes 4718596
  350.5 2.8 copy-start.14
  351.1 11.3 %slice-start = ((s8[4718592]{0:T(1024)(128)(4,1)}), s8[4194304]{0:T(1024)(128)(4,1)S(1)}, s32[]{:S(2)}) async-start(s8[4718592]{0:T(1024)(128)(4,1)} %bitcast.239), calls=%async_computation.19 | async-start | bytes 8388608
  351.7 10.7 %copy-start.8 = (f32[512,768]{1,0:T(8,128)}, f32[512,768]{1,0:T(8,128)S(1)}, u32[]{:S(2)}) copy-start(f32[512,768]{1,0:T(8,128)S(1)} %get-tuple-element.340) | copy-start | bytes 4718596
  353.2 9.2 copy-start.4
  353.2 9.2 slice-start.1
  367.6 1.7 copy-start.15
  368.1 1.1 copy-start.1
  496.0 140.5 %reduce-scatter.21.cloned.1.call-start = ((), (), s32[]{:S(2)}) async-start(), calls=%async_computation.16 | async-start | bytes 7077888
  514.0 187.1 %reduce-scatter.23.cloned.1.call-start = ((), (), s32[]{:S(2)}) async-start(), calls=%async_computation.17 | async-start | bytes 4423680
  639.8 4.3 copy-start.16
  655.4 77.1 %reduce-scatter.13.cloned.1.call-start = ((), (), s32[]{:S(2)}) async-start(), calls=%async_computation.12 | async-start | bytes 1474560 | tf_op jit(solution)/shard_map/reduce_scatter | solution.py:286
  658.9 133.7 %reduce-scatter.15.cloned.1.call-start = ((), (), s32[]{:S(2)}) async-start(), calls=%async_computation.13 | async-start | bytes 5898240 | tf_op jit(solution)/shard_map/reduce_scatter | solution.py:298
  667.1 185.5 %reduce-scatter.17.cloned.1.call-start = ((), (), s32[]{:S(2)}) async-start(), calls=%async_computation.14 | async-start | bytes 5898240 | tf_op jit(solution)/shard_map/reduce_scatter | solution.py:304
  674.6 273.0 %all-reduce.23.cloned.1.call-start = ((), (), s32[]{:S(2)}) async-start(), calls=%async_computation.18 | async-start | bytes 7667712 | tf_op jit(solution)/shard_map/psum | solution.py:318
  703.4 150.6 %copy-start.17 = (bf16[192]{0:T(256)(128)(2,1)S(1)}, bf16[192]{0:T(256)(128)(2,1)}, u32[]{:S(2)}) copy-start(bf16[192]{0:T(256)(128)(2,1)} %param.35) | copy-start | bytes 1156
  856.1 37.7 %copy-start.2 = (f32[512,768]{1,0:T(8,128)S(1)}, f32[512,768]{1,0:T(8,128)}, u32[]{:S(2)}) copy-start(f32[512,768]{1,0:T(8,128)} %copy-done.1) | copy-start | bytes 4718596
  947.6 3.0 copy-start.9
  950.7 1.7 copy-start.10
  952.3 1.6 copy-start.11
Sparse Core Ops, SparseCore 0:
  9.9 50.0 all-gather.7
  67.7 65.1 all-gather.11
  135.0 63.2 all-gather.9
  200.1 25.9 all-gather.13
  227.7 57.1 all-gather.15
  286.6 57.0 all-gather.17
  496.1 69.7 reduce-scatter.18
  568.2 68.1 reduce-scatter.20
  655.5 45.5 reduce-scatter.22
  703.9 28.5 reduce-scatter.12
  735.5 57.0 reduce-scatter.14
  795.4 57.0 reduce-scatter.16
  855.8 91.8 all-reduce.22
where the time goes:
time: 970 us; the launch traced here: 961 us
  waiting for transfers between devices  527 us (54%)
  matrix products  222 us (23%)
  local copies, waits for them, and re-layouts  98.2 us (10%)
  blocking collectives  68.6 us (7%)
  other arithmetic  27.7 us (3%)
  between operations  16.5 us (2%)
    unnamed x16, waiting for transfers between devices  145 us
    unnamed x81, local copies, waits for them, and re-layouts  80.3 us
    reduce_scatter x1, waiting for transfers between devices, on_device(): lax.psum_scatter(grad_inner_weight.astype(jnp.bfloat16), 'seq', scatter_d...  60.1 us
    reduce_scatter x1, waiting for transfers between devices, on_device(): lax.psum_scatter(grad_outer_weight.astype(jnp.bfloat16), 'seq', scatter_d...  60 us
    all_gather x1, waiting for transfers between devices, on_device(): key_part = lax.all_gather(keys_low, 'ctx', axis=1, tiled=True)  58.8 us
    psum x1, waiting for transfers between devices, on_device(): lax.psum(owned[0].astype(jnp.bfloat16), 'ctx').astype(jnp.float32)  47.9 us
    all_gather x1, waiting for transfers between devices, on_device(): lax.all_gather(outer_weight, 'seq', axis=0, tiled=True)  39 us
    all_gather x1, waiting for transfers between devices, on_device(): value_part = lax.all_gather(values_low, 'ctx', axis=1, tiled=True)  36.3 us
  transfers between devices with their start and end apart: 13, of which 12 were waited for; matrix products, arithmetic and copies ran while one was open for 17% of the time, Pallas kernels for 0%

commit v1 on v0

--- a/solution.py
+++ b/solution.py
@@ -7,6 +7,28 @@
 HEADS = 12
 HEAD_DIM = 64
 norm_epsilon = 1e-12
+
+
+def find_plate(piece_in, dim_at):
+    shard_axis = "seq"
+    known, work_now, met_up = (
+        lax.psum(1, shard_axis),
+        lax.axis_index(shard_axis),
+        piece_in.shape[dim_at],
+    )
+    z1, long_array = (piece_in, 1)
+    while long_array < known:
+        z1 = jnp.concatenate(
+            [
+                z1,
+                lax.ppermute(
+                    z1, shard_axis, [(rr, (rr - long_array) % known) for rr in range(known)]
+                ),
+            ],
+            axis=dim_at,
+        )
+        long_array = 2 * long_array
+    return jnp.roll(z1, shift=work_now * met_up, axis=dim_at)
 
 
 def norm_forward(matrix, gain, shift):
@@ -85,7 +107,7 @@
     row_count = groups * positions
     scaling = HEAD_DIM ** (-0.5)
     gathered = (
-        lax.all_gather(qkv_weight, "seq", axis=0, tiled=True),
+        find_plate(qkv_weight, 0),
         lax.all_gather(query_bias, "seq", axis=0, tiled=True),
         lax.all_gather(value_bias, "seq", axis=0, tiled=True),
         lax.all_gather(out_weight, "seq", axis=0, tiled=True),

time: 970 us -> 1030 us (1.062)
  waiting for transfers between devices: 527 us -> 580 us
    psum x1, waiting for transfers between devices: 47.9 us -> 88.6 us  [on_device(): lax.psum(owned[0].astype(jnp.bfloat16), 'ctx').astype(jnp.float32)]
    ppermute x0 -> x2, waiting for transfers between devices: none -> 30.1 us  [find_plate(): lax.ppermute(z1, shard_axis, [(rr, (rr - long_array) % known) for rr in r...]
    all_gather x1, waiting for transfers between devices: 26.3 us -> 8.85 us  [on_device(): lax.all_gather(qkv_weight, 'seq', axis=0, tiled=True)]
    unnamed x81 -> x108, local copies, waits for them, and re-layouts: 80.3 us -> 82.4 us
  transfers between devices with their start and end apart: 13 -> 15, of which waited for: 12 -> 14; matrix products, arithmetic and copies ran while one was open for 17% -> 16% of each run, Pallas kernels for 0% -> 0%
where the time goes in v1:
time: 1030 us; the launch traced here: 1020 us
  waiting for transfers between devices  580 us (56%)
  matrix products  220 us (21%)
  local copies, waits for them, and re-layouts  100 us (10%)
  blocking collectives  68.5 us (7%)
  other arithmetic  31.5 us (3%)
  between operations  16.7 us (2%)
    unnamed x16, waiting for transfers between devices  145 us
    psum x1, waiting for transfers between devices, on_device(): lax.psum(owned[0].astype(jnp.bfloat16), 'ctx').astype(jnp.float32)  88.6 us
    unnamed x108, local copies, waits for them, and re-layouts  82.4 us
    reduce_scatter x1, waiting for transfers between devices, on_device(): lax.psum_scatter(grad_inner_weight.astype(jnp.bfloat16), 'seq', scatter_d...  60.1 us
    reduce_scatter x1, waiting for transfers between devices, on_device(): lax.psum_scatter(grad_outer_weight.astype(jnp.bfloat16), 'seq', scatter_d...  60 us
    all_gather x1, waiting for transfers between devices, on_device(): key_part = lax.all_gather(keys_low, 'ctx', axis=1, tiled=True)  58.9 us
    all_gather x1, waiting for transfers between devices, on_device(): lax.all_gather(outer_weight, 'seq', axis=0, tiled=True)  38.9 us
    all_gather x1, waiting for transfers between devices, on_device(): value_part = lax.all_gather(values_low, 'ctx', axis=1, tiled=True)  37 us
  transfers between devices with their start and end apart: 15, of which 14 were waited for; matrix products, arithmetic and copies ran while one was open for 16% of the time, Pallas kernels for 0%

profile of v1, /device:TPU:0, one launch (start us, length us, event | category | flops | bytes accessed | tf_op | source)
XLA Modules:
  0.0 1024.7 jit_solution(10444486896741572741)
XLA Ops:
  7.3 3.9 collective-permute-start
  11.2 19.2 %collective-permute-done = bf16[192,2304]{1,0:T(8,128)(2,1)S(1)} collective-permute-done((bf16[192,2304]{1,0:T(8,128)(2,1)}, bf16[192,2304]{1,0:T(8,128)(2,1)S(1)}, u32[]{:S(2)}, u32[]{:S(2)}) %collective-permute-start) | collective-permute-done | bytes 884768 | tf_op jit(solution)/shard_map/ppermute | solution.py:24
  30.4 2.5 pad_maximum_fusion
  43.0 17.6 %all-reduce.20 = (bf16[768]{0:T(1024)(128)(2,1)}, bf16[768]{0:T(1024)(128)(2,1)}, bf16[768]{0:T(1024)(128)(2,1)}, bf16[768]{0:T(1024)(128)(2,1)}, bf16[768]{0:T(...) all-reduce(bf16[768]{0:T(1024)(128)(2,1)S(1)} %dynamic-update-slice, ...), channel_id=1, replica_groups=mesh['seq'=4,'ctx'=8] {'seq'}, use_global_device_ids=true, to_apply=%add | all-reduce | flops 5376 | bytes 21504
  62.1 10.9 %collective-permute-done.1 = bf16[384,2304]{1,0:T(8,128)(2,1)S(1)} collective-permute-done((bf16[384,2304]{1,0:T(8,128)(2,1)}, bf16[384,2304]{1,0:T(8,128)(2,1)S(1)}, u32[]{:S(2)}, u32[]{:S(2)}) %collective-permute-start.1) | collective-permute-done | bytes 1769504 | tf_op jit(solution)/shard_map/ppermute | solution.py:24
  74.3 2.0 convolution_bitcast_fusion.1
  84.5 12.1 %all_gather.58 = bf16[4,1024]{1,0:T(4,128)(2,1)S(1)} all-gather(bf16[4,128]{1,0:T(4,128)(2,1)S(1)} %convert_element_type.236), channel_id=1, replica_groups=mesh['seq'=4,'ctx'=8] {'ctx'}, dimensions={1}, use_global_device_ids=true | all-gather | bytes 9216 | tf_op jit(solution)/shard_map/all_gather | solution.py:165
  96.6 8.9 all-gather
  109.8 37.0 %all-gather.10.cloned.1.call-done = bf16[4,1024,768]{1,2,0:T(8,128)(2,1)} async-done(((bf16[4,128,768]{1,2,0:T(8,128)(2,1)}), bf16[4,1024,768]{1,2,0:T(8,128)(2,1)}) %all-gather.10.cloned.1.call-update) | async-done | bytes 6291472 | tf_op jit(solution)/shard_map/all_gather | solution.py:164
  146.9 6.7 copy.57
  153.6 58.9 %all-gather.8.cloned.1.call-done = bf16[4,1024,768]{1,2,0:T(8,128)(2,1)} async-done(((bf16[4,128,768]{1,2,0:T(8,128)(2,1)}), bf16[4,1024,768]{1,2,0:T(8,128)(2,1)}) %all-gather.8.cloned.1.call-update) | async-done | bytes 6291472 | tf_op jit(solution)/shard_map/all_gather | solution.py:163
  212.4 6.7 copy.56
  219.1 51.8 %while.30 = (s32[]{:T(128)}, f32[12,4,128]{2,1,0:T(4,128)S(1)}, f32[12,4,128]{2,1,0:T(4,128)S(1)}, f32[12,4,128,64]{2,1,3,0:T(4,128)S(1)}, bf16[12,4,128,64]{2,3...) while((s32[]{:T(128)}, f32[12,4,128]{2,1,0:T(4,128)S(1)}, ...), condition=%wide.region_3.4_spmd.clone, body=%wide.region_0.3_spmd.clone.sunk | while | flops 142641664 | bytes 7852653 | solution.py:187
  272.0 2.7 fusion.85
  275.0 24.0 %all-gather.14.cloned.1.call-done = bf16[768,3072]{1,0:T(8,128)(2,1)} async-done(((bf16[192,3072]{1,0:T(8,128)(2,1)}), bf16[768,3072]{1,0:T(8,128)(2,1)}) %all-gather.14.cloned.1.call-update) | async-done | bytes 4718608 | tf_op jit(solution)/shard_map/all_gather | solution.py:117
  299.0 19.8 %multiply_convert_fusion.1 = (bf16[512,3072]{1,0:T(8,128)(2,1)}, f32[512,3072]{1,0:T(8,128)}, f32[512,3072]{1,0:T(8,128)}) fusion(f32[3072]{0:T(1024)S(1)} %bitcast.238, bf16[768,3072]{1,0:T(8,128)(2,1)} %all-gather.14.cloned.1.call-done, f32[512,768]{1,0:T(8,128)S(1)} %get-tuple-element.358, f32[768]{0:T(1024)S(1)} %convert_element_type.244, ...), kind=kOutput, calls=%fused_computation.66 | convolution fusion | flops 2521694208 | bytes 22042624 | tf_op jit(solution)/shard_map/dot_general | solution.py:205
  318.9 38.9 %all-gather.16.cloned.1.call-done = bf16[3072,768]{1,0:T(8,128)(2,1)} async-done(((bf16[768,768]{1,0:T(8,128)(2,1)}), bf16[3072,768]{1,0:T(8,128)(2,1)}) %all-gather.16.cloned.1.call-update) | async-done | bytes 4718608 | tf_op jit(solution)/shard_map/all_gather | solution.py:119
  357.8 6.5 fusion.86
  367.4 9.2 fusion.87
  376.6 5.1 multiply_reduce_fusion
  389.1 103.7 %while.31 = (s32[]{:T(128)}, bf16[12,4,128,64]{2,3,1,0:T(8,128)(2,1)}, bf16[12,4,1024,64]{2,3,0,1:T(8,128)(2,1)}, bf16[12,4,1024,64]{2,3,0,1:T(8,128)(2,1)}, bf1...) while((s32[]{:T(128)}, ...), condition=%wide.region_14.15_spmd.clone, body=%wide.region_13.14_spmd.clone.sunk | while | flops 340033536 | bytes 13657221 | solution.py:266
  396.0 2.2 fusion.138
  404.6 2.2 fusion.138
  410.1 2.0 fusion.139
  413.2 2.2 fusion.138
  421.8 2.2 fusion.138
  430.4 2.2 fusion.138
  439.0 2.2 fusion.138
  444.5 2.0 fusion.139
  447.6 2.2 fusion.138
  456.2 2.2 fusion.138
  464.8 2.2 fusion.138
  470.3 2.0 fusion.139
  473.4 2.2 fusion.138
  478.9 2.0 fusion.139
  482.0 2.2 fusion.138
  487.6 2.0 fusion.139
  490.7 2.2 fusion.138
  492.8 10.8 %copy.70 = bf16[4,1024,768]{2,0,1:T(4,128)(2,1)} copy(bf16[4,1024,768]{1,2,0:T(8,128)(2,1)} %bitcast.220) | data formatting | bytes 12582912
  503.6 6.9 copy.100
  510.6 11.0 %copy.72 = bf16[4,1024,768]{2,0,1:T(4,128)(2,1)} copy(bf16[4,1024,768]{1,2,0:T(8,128)(2,1)} %bitcast.221) | data formatting | bytes 12582912
  521.6 7.0 copy.102
  531.4 49.1 %reduce-scatter.19.cloned.1.call-done = bf16[128,3072]{1,0:T(8,128)(2,1)} async-done(((bf16[1024,3072]{1,0:T(8,128)(2,1)}), bf16[128,3072]{1,0:T(8,128)(2,1)}) %reduce-scatter.19.cloned.1.call-update) | async-done | bytes 786448
  580.5 2.0 reshape.221
  583.8 67.2 %reduce-scatter.21.cloned.1.call-done = bf16[128,3072]{1,0:T(8,128)(2,1)} async-done(((bf16[1024,3072]{1,0:T(8,128)(2,1)}), bf16[128,3072]{1,0:T(8,128)(2,1)}) %reduce-scatter.21.cloned.1.call-update) | async-done | bytes 786448
  651.0 2.0 reshape.223
  654.4 2.2 bitcast_dynamic-update-slice_fusion.2
  656.6 2.1 bitcast_dynamic-update-slice_fusion.1
  658.7 5.4 fusion.54
  664.1 5.8 copy.74
  669.9 3.5 convolution_convert_fusion.3
  673.7 7.7 convolution_convert_fusion
  681.5 7.6 convolution_convert_fusion.1
  689.7 25.9 %reduce-scatter.23.cloned.1.call-done = bf16[192,2304]{1,0:T(8,128)(2,1)} async-done(((bf16[768,2304]{1,0:T(8,128)(2,1)}), bf16[192,2304]{1,0:T(8,128)(2,1)}) %reduce-scatter.23.cloned.1.call-update) | async-done | bytes 884752
  715.6 2.3 copy.75
  718.0 29.2 %reduce-scatter.13.cloned.1.call-done = bf16[192,768]{1,0:T(8,128)(2,1)} async-done(((bf16[768,768]{1,0:T(8,128)(2,1)}), bf16[192,768]{1,0:T(8,128)(2,1)}) %reduce-scatter.13.cloned.1.call-update) | async-done | bytes 294928 | tf_op jit(solution)/shard_map/reduce_scatter | solution.py:308
  747.1 60.0 %reduce-scatter.17.cloned.1.call-done = bf16[768,768]{1,0:T(8,128)(2,1)} async-done(((bf16[3072,768]{1,0:T(8,128)(2,1)}), bf16[768,768]{1,0:T(8,128)(2,1)}) %reduce-scatter.17.cloned.1.call-update) | async-done | bytes 1179664 | tf_op jit(solution)/shard_map/reduce_scatter | solution.py:326
  807.1 60.1 %reduce-scatter.15.cloned.1.call-done = bf16[192,3072]{1,0:T(8,128)(2,1)} async-done(((bf16[768,3072]{1,0:T(8,128)(2,1)}), bf16[192,3072]{1,0:T(8,128)(2,1)}) %reduce-scatter.15.cloned.1.call-update) | async-done | bytes 1179664 | tf_op jit(solution)/shard_map/reduce_scatter | solution.py:320
  870.8 16.0 %all-reduce.19 = (bf16[768]{0:T(1024)(128)(2,1)S(1)}, bf16[768]{0:T(1024)(128)(2,1)S(1)}, bf16[768]{0:T(1024)(128)(2,1)S(1)}, bf16[768]{0:T(1024)(128)(2,1)S(1)}...) all-reduce(bf16[768]{0:T(1024)(128)(2,1)S(1)} %dynamic-update-slice, ...), channel_id=1, replica_groups=mesh['seq'=4,'ctx'=8] {'seq'}, use_global_device_ids=true, to_apply=%add.7 | all-reduce | flops 9984 | bytes 39936
  887.5 13.9 %all-reduce.17 = (bf16[192]{0:T(256)(128)(2,1)S(1)}, bf16[192]{0:T(256)(128)(2,1)S(1)}, bf16[192]{0:T(256)(128)(2,1)S(1)}, bf16[192]{0:T(256)(128)(2,1)S(1)}, bf...) all-reduce(bf16[192]{0:T(256)(128)(2,1)S(1)} %dynamic-slice.9, ...), channel_id=1, replica_groups=mesh['seq'=4,'ctx'=8] {'ctx'}, use_global_device_ids=true, to_apply=%region_21.22 | all-reduce | flops 2304 | bytes 9216 | tf_op jit(solution)/shard_map/psum | solution.py:341
  907.6 8.8 all-gather.18.cloned.1.call-done
  916.5 5.9 convolution_add_fusion.1
  922.4 88.6 %all-reduce.23.cloned.1.call-done = (bf16[192,2304]{0,1:T(8,128)(2,1)}, bf16[192,768]{1,0:T(8,128)(2,1)}, bf16[192,3072]{1,0:T(8,128)(2,1)}, bf16[768,768]{1,0:T(8,128)(2,1)}) async-done(((bf16[192,2304]{0,1:T(8,128)(2,1)}, bf16[192,768]{1,0:T(8,128)(2,1)}, bf16[192,3072]{1,0:T(8,128)(2,1)}, bf16[768,768]{1,0:T(8,128)(2,1)}), (bf16[192,2304]{0,1:T(8,128)(2,1)}, bf16[192,768]{1,0:T(8,128)(2,1)}, ...) | async-done | bytes 3538960 | tf_op jit(solution)/shard_map/psum | solution.py:340
  1011.0 3.0 convert_element_type.284
  (326 shorter events, 174.5 us)
Async XLA Ops:
  7.2 27.2 %copy-start.18 = (u32[32]{0:T(128)S(1)}, u32[32]{0:T(128)}, u32[]{:S(2)}) copy-start(u32[32]{0:T(128)} %constant.166) | copy-start | bytes 388
  7.2 54.8 %copy-start = (bf16[192,2304]{1,0:T(8,128)(2,1)S(1)}, bf16[192,2304]{1,0:T(8,128)(2,1)}, u32[]{:S(2)}) copy-start(bf16[192,2304]{1,0:T(8,128)(2,1)} %param.23) | copy-start | bytes 2654212
  7.2 28.4 %copy-start.25 = (bf16[192]{0:T(256)(128)(2,1)S(1)}, bf16[192]{0:T(256)(128)(2,1)}, u32[]{:S(2)}) copy-start(bf16[192]{0:T(256)(128)(2,1)} %param.24) | copy-start | bytes 1156
  7.2 28.7 %copy-start.26 = (bf16[192]{0:T(256)(128)(2,1)S(1)}, bf16[192]{0:T(256)(128)(2,1)}, u32[]{:S(2)}) copy-start(bf16[192]{0:T(256)(128)(2,1)} %param.25) | copy-start | bytes 1156
  7.2 28.9 %copy-start.27 = (bf16[192]{0:T(256)(128)(2,1)S(1)}, bf16[192]{0:T(256)(128)(2,1)}, u32[]{:S(2)}) copy-start(bf16[192]{0:T(256)(128)(2,1)} %param.27) | copy-start | bytes 1156
  7.2 139.6 %all-gather.10.cloned.1.call-start = ((), (), s32[]{:S(2)}) async-start(), calls=%async_computation.7 | async-start | bytes 7077888 | tf_op jit(solution)/shard_map/all_gather | solution.py:164
  7.3 23.2 %collective-permute-start = (bf16[192,2304]{1,0:T(8,128)(2,1)}, bf16[192,2304]{1,0:T(8,128)(2,1)S(1)}, u32[]{:S(2)}, u32[]{:S(2)}) collective-permute-start(bf16[192,2304]{1,0:T(8,128)(2,1)} %param.23), channel_id=1, source_target_pairs={{0,24},{8,0},{16,8},{24,16},{1,25},{9,1},{17,9},{25,17},{2,26},{10... | collective-permute-start | bytes 2654216 | tf_op jit(solution)/shard_map/ppermute | solution.py:24
  32.9 40.0 %collective-permute-start.1 = (bf16[384,2304]{1,0:T(8,128)(2,1)}, bf16[384,2304]{1,0:T(8,128)(2,1)S(1)}, u32[]{:S(2)}, u32[]{:S(2)}) collective-permute-start(bf16[384,2304]{1,0:T(8,128)(2,1)} %pad_maximum_fusion), channel_id=1, source_target_pairs={{0,16},{8,24},{16,0},{24,8},{1,17},{9,25},{17,1},{25,9},{2,18},{10... | collective-permute-start | bytes 5308424 | tf_op jit(solution)/shard_map/ppermute | solution.py:24
  73.2 1.1 copy-start.23
  76.3 2.1 copy-start.7
  79.6 132.8 %all-gather.8.cloned.1.call-start = ((), (), s32[]{:S(2)}) async-start(), calls=%async_computation.6 | async-start | bytes 7077888 | tf_op jit(solution)/shard_map/all_gather | solution.py:163
  81.2 3.3 copy-start.19
  81.2 15.4 %copy-start.17 = (bf16[768]{0:T(1024)(128)(2,1)S(1)}, bf16[768]{0:T(1024)(128)(2,1)}, u32[]{:S(2)}) copy-start(bf16[768]{0:T(1024)(128)(2,1)} %get-tuple-element.334) | copy-start | bytes 4612
  81.2 15.3 %copy-start.16 = (bf16[768]{0:T(1024)(128)(2,1)S(1)}, bf16[768]{0:T(1024)(128)(2,1)}, u32[]{:S(2)}) copy-start(bf16[768]{0:T(1024)(128)(2,1)} %get-tuple-element.336) | copy-start | bytes 4612
  81.2 15.3 %copy-start.15 = (bf16[768]{0:T(1024)(128)(2,1)S(1)}, bf16[768]{0:T(1024)(128)(2,1)}, u32[]{:S(2)}) copy-start(bf16[768]{0:T(1024)(128)(2,1)} %get-tuple-element.335) | copy-start | bytes 4612
  81.2 15.4 %copy-start.20 = (bf16[768]{0:T(1024)(128)(2,1)S(1)}, bf16[768]{0:T(1024)(128)(2,1)}, u32[]{:S(2)}) copy-start(bf16[768]{0:T(1024)(128)(2,1)} %param.31) | copy-start | bytes 4612
  81.2 24.3 %copy-start.14 = (bf16[768]{0:T(1024)(128)(2,1)S(1)}, bf16[768]{0:T(1024)(128)(2,1)}, u32[]{:S(2)}) copy-start(bf16[768]{0:T(1024)(128)(2,1)} %get-tuple-element.337) | copy-start | bytes 4612
  81.2 24.3 %copy-start.13 = (bf16[768]{0:T(1024)(128)(2,1)S(1)}, bf16[768]{0:T(1024)(128)(2,1)}, u32[]{:S(2)}) copy-start(bf16[768]{0:T(1024)(128)(2,1)} %get-tuple-element.338) | copy-start | bytes 4612
  81.3 24.3 %copy-start.1 = (bf16[4,128,768]{2,1,0:T(8,128)(2,1)S(1)}, bf16[4,128,768]{2,1,0:T(8,128)(2,1)}, u32[]{:S(2)}) copy-start(bf16[4,128,768]{2,1,0:T(8,128)(2,1)} %param.21) | copy-start | bytes 2359300
  82.4 188.8 %all-gather.12.cloned.1.call-start = ((), (), s32[]{:S(2)}) async-start(), calls=%async_computation.8 | async-start | bytes 1474560 | tf_op jit(solution)/shard_map/all_gather | solution.py:113
  83.2 215.9 %all-gather.14.cloned.1.call-start = ((), (), s32[]{:S(2)}) async-start(), calls=%async_computation.9 | async-start | bytes 5898240 | tf_op jit(solution)/shard_map/all_gather | solution.py:117
  83.8 274.1 %all-gather.16.cloned.1.call-start = ((), (), s32[]{:S(2)}) async-start(), calls=%async_computation.10 | async-start | bytes 5898240 | tf_op jit(solution)/shard_map/all_gather | solution.py:119
  84.3 496.1 %reduce-scatter.19.cloned.1.call-start = ((), (), s32[]{:S(2)}) async-start(), calls=%async_computation.15 | async-start | bytes 7077888
  270.9 1.1 copy-start.6
  271.3 3.4 copy-start.8
  274.7 44.2 %copy-start.4 = (f32[512,768]{1,0:T(8,128)}, f32[512,768]{1,0:T(8,128)S(1)}, u32[]{:S(2)}) copy-start(f32[512,768]{1,0:T(8,128)S(1)} %get-tuple-element.358) | copy-start | bytes 4718596
  364.6 2.8 copy-start.21
  365.3 11.3 %slice-start = ((s8[4718592]{0:T(1024)(128)(4,1)}), s8[4194304]{0:T(1024)(128)(4,1)S(1)}, s32[]{:S(2)}) async-start(s8[4718592]{0:T(1024)(128)(4,1)} %bitcast.240), calls=%async_computation.19 | async-start | bytes 8388608
  365.9 10.7 %copy-start.9 = (f32[512,768]{1,0:T(8,128)}, f32[512,768]{1,0:T(8,128)S(1)}, u32[]{:S(2)}) copy-start(f32[512,768]{1,0:T(8,128)S(1)} %get-tuple-element.340) | copy-start | bytes 4718596
  367.4 9.2 copy-start.5
  367.4 9.2 slice-start.1
  381.8 1.7 copy-start.22
  382.3 1.1 copy-start.2
  510.5 140.5 %reduce-scatter.21.cloned.1.call-start = ((), (), s32[]{:S(2)}) async-start(), calls=%async_computation.16 | async-start | bytes 7077888
  528.6 187.0 %reduce-scatter.23.cloned.1.call-start = ((), (), s32[]{:S(2)}) async-start(), calls=%async_computation.17 | async-start | bytes 4423680
  654.4 4.3 copy-start.24
  669.9 77.2 %reduce-scatter.13.cloned.1.call-start = ((), (), s32[]{:S(2)}) async-start(), calls=%async_computation.12 | async-start | bytes 1474560 | tf_op jit(solution)/shard_map/reduce_scatter | solution.py:308
  673.5 133.7 %reduce-scatter.17.cloned.1.call-start = ((), (), s32[]{:S(2)}) async-start(), calls=%async_computation.14 | async-start | bytes 5898240 | tf_op jit(solution)/shard_map/reduce_scatter | solution.py:326
  681.4 185.8 %reduce-scatter.15.cloned.1.call-start = ((), (), s32[]{:S(2)}) async-start(), calls=%async_computation.13 | async-start | bytes 5898240 | tf_op jit(solution)/shard_map/reduce_scatter | solution.py:320
  689.1 227.4 %all-gather.18.cloned.1.call-start = ((), (), s32[]{:S(2)}) async-start(), calls=%async_computation.11 | async-start | bytes 4423680 | tf_op jit(solution)/shard_map/all_gather | solution.py:211
  689.7 321.3 %all-reduce.23.cloned.1.call-start = ((), (), s32[]{:S(2)}) async-start(), calls=%async_computation.18 | async-start | bytes 7667712 | tf_op jit(solution)/shard_map/psum | solution.py:340
  718.0 150.8 %copy-start.28 = (bf16[192]{0:T(256)(128)(2,1)S(1)}, bf16[192]{0:T(256)(128)(2,1)}, u32[]{:S(2)}) copy-start(bf16[192]{0:T(256)(128)(2,1)} %param.35) | copy-start | bytes 1156
  870.8 45.7 %copy-start.3 = (f32[512,768]{1,0:T(8,128)S(1)}, f32[512,768]{1,0:T(8,128)}, u32[]{:S(2)}) copy-start(f32[512,768]{1,0:T(8,128)} %copy-done.2) | copy-start | bytes 4718596
  1010.9 3.0 copy-start.10
  1014.0 1.7 copy-start.11
  1015.6 1.6 copy-start.12
Sparse Core Ops, SparseCore 0:
  79.8 67.0 all-gather.9
  149.0 63.3 all-gather.7
  214.3 25.9 all-gather.11
  241.9 57.0 all-gather.13
  300.7 57.0 all-gather.15
  510.7 69.7 reduce-scatter.18
  582.8 68.1 reduce-scatter.20
  670.0 45.5 reduce-scatter.22
  718.6 28.5 reduce-scatter.12
  750.0 57.0 reduce-scatter.16
  810.1 57.0 reduce-scatter.14
  868.9 47.4 all-gather.17
  919.7 91.2 all-reduce.22
